TPU v7x, 32 devices: a whole 2x2x4 slice. The times are simulated.
32 devices in a mesh: ckpt: 4 (over z), shard: 8 (over y, x, core).
Axes of the slice: x: 2, y: 2, z: 4, core: 2. Of those that a mesh axis runs over, the one named last changes fastest.
Arguments:
- task_vectors: bfloat16 [4, 4096, 16384], P('ckpt', 'shard'), may hold values from -0.125 to 0.125, as said below
- thresholds: float32 [4], replicated, may hold values from 0.009 to 0.062, as said below
- base_weight: float32 [4096, 16384], P('ckpt', 'shard'), may hold values from -0.3 to 0.3
Outputs:
- merged: float32 [4096, 16384], P('ckpt', 'shard')
Inputs may be any that keep to these rules, and one draw needn't show every extreme that they name: `task_vectors`: every entry is a whole multiple of 2^-14. `thresholds`: every threshold is an odd multiple of 2^-15.
All inputs are finite; a program needn't handle non-finite values.
Results may differ from a plain program's by a relative error of at most 0.0003.
Values may be sent and summed in bfloat16 or wider, within the bound.
A program may use at most 128 MiB of HBM per device.

v0:
```python
import jax
import jax.numpy as jnp
from jax import lax
from jax.sharding import PartitionSpec as P


def local_mean(all_tasks, limits):
    values = all_tasks.astype(jnp.float32)
    trimmed = jnp.where(jnp.abs(values) > limits[:, None, None], values, jnp.float32(0.0))
    signed_total = jnp.sum(trimmed, axis=0)
    agreeing = jnp.logical_or(
        jnp.logical_and(signed_total[None] > 0, trimmed > 0),
        jnp.logical_and(signed_total[None] < 0, trimmed < 0),
    )
    kept_sum = jnp.sum(jnp.where(agreeing, trimmed, jnp.float32(0.0)), axis=0)
    agree_count = jnp.sum(agreeing.astype(jnp.float32), axis=0)
    return jnp.where(agree_count > 0, kept_sum / jnp.maximum(agree_count, 1.0), jnp.float32(0.0))


def local(task_vectors, thresholds, base_weight):
    ckpt_count = lax.axis_size("ckpt")
    shard_count = lax.axis_size("shard")
    all_tasks = lax.all_to_all(task_vectors, "ckpt", split_axis=1, concat_axis=0, tiled=True)
    mean_part = local_mean(all_tasks, thresholds)
    block_rows = mean_part.shape[0]
    by_columns = lax.all_to_all(mean_part, "shard", split_axis=1, concat_axis=0, tiled=True)
    col_width = by_columns.shape[1]
    by_rows = lax.all_to_all(by_columns, "ckpt", split_axis=0, concat_axis=0, tiled=True)
    group_size = shard_count // ckpt_count
    disjoint = by_rows.reshape(ckpt_count, group_size, block_rows, col_width)
    disjoint = disjoint.transpose(1, 0, 2, 3).reshape(
        group_size * ckpt_count * block_rows, col_width
    )
    return base_weight + disjoint


def solution(mesh):
    placed = (P("ckpt", "shard", None), P(), P("ckpt", "shard"))
    return jax.shard_map(
        local, mesh=mesh, in_specs=placed, out_specs=P("ckpt", "shard"), check_vma=False
    )
```

profile of v0, /device:TPU:0, one launch (start us, length us, event | category | flops | bytes accessed | tf_op | source)
XLA Modules:
  0.0 955.8 jit_solution(856141177414765462)
XLA Ops:
  0.0 29.1 %copy.18 = bf16[1,512,16384]{2,0,1:T(2,128)(2,1)} copy(bf16[1,512,16384]{2,1,0:T(8,128)(2,1)} %param.3) | data formatting | bytes 33554432 | tf_op args[0]
  29.1 0.5 broadcast.94
  29.6 99.6 %reduce = bf16[512,16384]{1,0:T(8,128)(2,1)} reduce(bf16[512,1,16384]{2,1,0:T(2,128)(2,1)} %bitcast.16, bf16[]{:T(256)} %broadcast.94), dimensions={1}, to_apply=%bitcast.13.reduce_sub_computation | reduce | bytes 33554432
  129.3 17.4 %reshape.60 = bf16[4,2,1048576]{2,1,0:T(2,128)(2,1)} reshape(bf16[512,16384]{1,0:T(8,128)(2,1)} %reduce) | data formatting | bytes 33554432
  146.6 375.8 %all_to_all.31 = bf16[4,2,1048576]{2,1,0:T(2,128)(2,1)} all-to-all(bf16[4,2,1048576]{2,1,0:T(2,128)(2,1)} %reshape.60), channel_id=1, replica_groups=mesh['ckpt'=4,'shard'=8] {'ckpt'}, dimensions={0} | all-to-all | bytes 33554432 | tf_op jit(solution)/shard_map/all_to_all | solution.py:23
  522.4 35.6 %reshape.61 = bf16[512,1,16384]{2,1,0:T(2,128)(2,1)} reshape(bf16[4,2,1048576]{2,1,0:T(2,128)(2,1)} %all_to_all.31) | data formatting | bytes 33554432
  558.0 0.0 copy-start
  558.1 28.2 %copy.13 = bf16[1,512,16384]{2,1,0:T(8,128)(2,1)S(1)} copy(bf16[1,512,16384]{2,0,1:T(2,128)(2,1)} %bitcast.17) | data formatting | bytes 33554432 | tf_op jit(solution)/shard_map/all_to_all | solution.py:23
  586.3 0.0 copy-done
  586.3 13.3 %fusion.3 = f32[128,16384]{1,0:T(8,128)S(1)} fusion(bf16[4,128,16384]{2,1,0:T(8,128)(2,1)S(1)} %bitcast.14, f32[4]{0:T(128)S(1)} %copy-done), kind=kLoop, calls=%fused_computation.5 | loop fusion | flops 39845888 | bytes 25165840 | tf_op jit(solution)/shard_map/reduce_sum | solution.py:10
  599.6 3.8 broadcast_compare_fusion.1
  603.4 25.8 %convert_reduce_fusion = (f32[128,16384]{1,0:T(8,128)S(1)}, f32[128,16384]{1,0:T(8,128)}) fusion(f32[4]{0:T(128)S(1)} %copy-done, bf16[4,128,16384]{2,1,0:T(8,128)(2,1)S(1)} %bitcast.15, pred[128,16384]{1,0:T(8,128)(4,1)} %get-tuple-element.8, pred[128,16384]{1,0:T(8,128)(4,1)} %get-tuple-element.7), kind=kLoop, calls=%fused_computation.8 | loop fusion | flops 104857600 | bytes 37748752 | tf_op jit(solution)/shard_map/reduce_sum | solution.py:16
  629.1 6.3 divide_select_fusion
  635.4 9.0 copy.14
  644.4 99.7 %all_to_all.32 = f32[128,8,2048]{0,2,1:T(8,128)} all-to-all(f32[128,8,2048]{0,2,1:T(8,128)} %bitcast.18), channel_id=1, replica_groups=mesh['ckpt'=4,'shard'=8] {'shard'}, dimensions={1} | all-to-all | bytes 16777216 | tf_op jit(solution)/shard_map/all_to_all | solution.py:26
  744.1 9.1 copy.15
  753.3 186.9 %all_to_all.33 = f32[4,256,2048]{2,1,0:T(8,128)S(1)} all-to-all(f32[4,256,2048]{2,1,0:T(8,128)} %bitcast.20), channel_id=1, replica_groups=mesh['ckpt'=4,'shard'=8] {'ckpt'}, dimensions={0} | all-to-all | bytes 16777216 | tf_op jit(solution)/shard_map/all_to_all | solution.py:28
  940.1 3.8 copy.16
  943.9 11.9 %bitcast_add_fusion = f32[1024,2048]{1,0:T(8,128)} fusion(f32[1024,2048]{1,0:T(8,128)} %param.5, f32[2,4,128,2048]{3,2,1,0:T(8,128)} %copy.16), kind=kLoop, calls=%fused_computation.12 | loop fusion | flops 2097152 | bytes 25165824 | tf_op jit(solution)/shard_map/add | solution.py:34
Async XLA Ops:
  558.0 28.3 %copy-start = (f32[4]{0:T(128)S(1)}, f32[4]{0:T(128)}, u32[]{:S(2)}) copy-start(f32[4]{0:T(128)} %param.4) | copy-start | bytes 52
where the time goes:
time: 957 us; the launch traced here: 956 us
  blocking collectives  662 us (69%)
  other arithmetic  161 us (17%)
  local copies, waits for them, and re-layouts  133 us (14%)
    all_to_all x1, blocking collectives, local(): lax.all_to_all(task_vectors, 'ckpt', split_axis=1, concat_axis=0, tiled=T...  376 us
    all_to_all x1, blocking collectives, local(): lax.all_to_all(by_columns, 'ckpt', split_axis=0, concat_axis=0, tiled=True)  187 us
    all_to_all x1, blocking collectives, local(): lax.all_to_all(mean_part, 'shard', split_axis=1, concat_axis=0, tiled=True)  99.7 us
    unnamed x1, other arithmetic  99.6 us
    unnamed x6, local copies, waits for them, and re-layouts  82.6 us
    all_to_all x1, local copies, waits for them, and re-layouts, local(): lax.all_to_all(task_vectors, 'ckpt', split_axis=1, concat_axis=0, tiled=T...  28.2 us
    reduce_sum x1, other arithmetic, local_mean(): agree_count = jnp.sum(agreeing.astype(jnp.float32), axis=0)  25.8 us

commit v1 on v0

v1 whole, which is shorter than its diff:
```python
import functools

import jax
import jax.numpy as jnp
from jax import lax
from jax.experimental import pallas as pl
from jax.experimental.pallas import tpu as pltpu
from jax.sharding import PartitionSpec as P

MESH = pl.DeviceIdType.MESH
CHUNK = 16
AHEAD = 3
LAG = 2


def merge_kernel(
    T, S, R, cw,
    thr_ref, x_ref, base_ref, out_ref,
    stage, recv, buf,
    s1_send, s1_recv, s2_send, s2_recv, own_sem, base_sem, out_sem,
):
    g = S // T
    RB, W = stage.shape[1], stage.shape[2]
    N = RB // R
    t = lax.axis_index("ckpt")
    s = lax.axis_index("shard")

    own = pltpu.make_async_copy(
        x_ref.at[0, :, pl.ds(pl.multiple_of(s * W, W), W)], stage.at[s], own_sem
    )
    base_in = pltpu.make_async_copy(base_ref, buf, base_sem)
    own.start()
    base_in.start()

    barrier = pltpu.get_barrier_semaphore()
    for d in range(1, S):
        pl.semaphore_signal(
            barrier, inc=1, device_id=(t, lax.rem(s + d, S)), device_id_type=MESH
        )
    for d in range(1, T):
        pl.semaphore_signal(
            barrier, inc=1, device_id=(lax.rem(t + d, T), s), device_id_type=MESH
        )
    pl.semaphore_wait(barrier, S - 1 + T - 1)

    def rows_of(j):
        return pl.ds(pl.multiple_of(j * R, R), R)

    def plane_copy(j, d):
        c = lax.rem(s + d, S)
        return pltpu.make_async_remote_copy(
            src_ref=x_ref.at[0, rows_of(j), pl.ds(pl.multiple_of(c * W, W), W)],
            dst_ref=stage.at[s, rows_of(j)],
            send_sem=s1_send.at[j],
            recv_sem=s1_recv.at[j],
            device_id=(t, c),
            device_id_type=MESH,
        )

    def line_copy(j, d):
        k = lax.rem(t + d, T)
        return pltpu.make_async_remote_copy(
            src_ref=stage.at[pl.ds(k * g, g), rows_of(j)],
            dst_ref=recv.at[T - d - 1, :, rows_of(j)],
            send_sem=s2_send.at[j],
            recv_sem=s2_recv.at[j],
            device_id=(k, s),
            device_id_type=MESH,
        )

    def plane_start(j):
        for d in range(S - 1, 0, -1):
            plane_copy(j, d).start()

    def plane_wait(sem, j):
        part = stage.at[pl.ds(0, S - 1), rows_of(j)]
        pltpu.make_async_copy(part, part, sem.at[j]).wait()

    def line_wait(sem, j):
        part = recv.at[:, :, rows_of(j)]
        pltpu.make_async_copy(part, part, sem.at[j]).wait()

    limits = [thr_ref[lax.rem(t + d, T)] for d in range(T)]

    def mean_rows(j):
        rows = rows_of(j)

        def cols_step(q, carry):
            cols = pl.ds(pl.multiple_of(q * cw, cw), cw)
            for i in range(g):
                trimmed = []
                for d in range(T):
                    if d == 0:
                        v = stage[t * g + i, rows, cols]
                    else:
                        v = recv[d - 1, i, rows, cols]
                    v = v.astype(jnp.float32)
                    trimmed.append(jnp.where(jnp.abs(v) > limits[d], v, 0.0))
                total = functools.reduce(jnp.add, trimmed)
                kept = jnp.zeros_like(total)
                count = jnp.zeros_like(total)
                for v in trimmed:
                    agree = v * total > 0
                    kept = kept + jnp.where(agree, v, 0.0)
                    count = count + jnp.where(agree, 1.0, 0.0)
                buf[i, rows, cols] = buf[i, rows, cols] + kept / jnp.maximum(count, 1.0)
            return carry

        lax.fori_loop(0, W // cw, cols_step, 0)

    def finish(j):
        line_wait(s2_recv, j)
        mean_rows(j)
        pltpu.make_async_copy(
            buf.at[:, rows_of(j)], out_ref.at[:, rows_of(j)], out_sem
        ).start()

    ahead = min(AHEAD, N)
    for j in range(ahead):
        plane_start(j)
    own.wait()
    base_in.wait()

    def step(j, carry):
        @pl.when(j + ahead < N)
        def _():
            plane_start(j + ahead)

        plane_wait(s1_recv, j)
        for d in range(T - 1, 0, -1):
            line_copy(j, d).start()

        @pl.when(j >= LAG)
        def _():
            finish(j - LAG)

        return carry

    lax.fori_loop(0, N, step, 0)

    def tail(j, carry):
        finish(j)
        return carry

    lax.fori_loop(N - LAG, N, tail, 0)

    def drain(j, carry):
        plane_wait(s1_send, j)
        line_wait(s2_send, j)
        return carry

    lax.fori_loop(0, N, drain, 0)
    pltpu.make_async_copy(buf, out_ref, out_sem).wait()


def local(task_vectors, thresholds, base_weight):
    T = lax.axis_size("ckpt")
    S = lax.axis_size("shard")
    RB = task_vectors.shape[1]
    W = task_vectors.shape[2] // S
    g = S // T
    R = min(CHUNK, RB)
    N = RB // R
    merged = pl.pallas_call(
        functools.partial(merge_kernel, T, S, R, min(W, 256)),
        out_shape=jax.ShapeDtypeStruct((g, RB, W), jnp.float32),
        in_specs=[
            pl.BlockSpec(memory_space=pltpu.SMEM),
            pl.BlockSpec(memory_space=pl.ANY),
            pl.BlockSpec(memory_space=pl.ANY),
        ],
        out_specs=pl.BlockSpec(memory_space=pl.ANY),
        scratch_shapes=[
            pltpu.VMEM((S, RB, W), jnp.bfloat16),
            pltpu.VMEM((T - 1, g, RB, W), jnp.bfloat16),
            pltpu.VMEM((g, RB, W), jnp.float32),
            pltpu.SemaphoreType.DMA((N,)),
            pltpu.SemaphoreType.DMA((N,)),
            pltpu.SemaphoreType.DMA((N,)),
            pltpu.SemaphoreType.DMA((N,)),
            pltpu.SemaphoreType.DMA,
            pltpu.SemaphoreType.DMA,
            pltpu.SemaphoreType.DMA,
        ],
        compiler_params=pltpu.CompilerParams(
            collective_id=0, has_side_effects=True, vmem_limit_bytes=60 * 1024 * 1024
        ),
        name="merge_exchange",
    )(thresholds, task_vectors, base_weight.reshape(g, RB, W))
    return merged.reshape(base_weight.shape)


def solution(mesh):
    placed = (P("ckpt", "shard", None), P(), P("ckpt", "shard"))
    return jax.shard_map(
        local, mesh=mesh, in_specs=placed, out_specs=P("ckpt", "shard"), check_vma=False
    )
```

time: 957 us -> 390 us (0.41)
  blocking collectives: 662 us -> 0 us
  Pallas kernels: 0 us -> 382 us
  other arithmetic: 161 us -> 0 us
  local copies, waits for them, and re-layouts: 133 us -> 7.89 us
    all_to_all x3 -> x0, blocking collectives: 662 us -> none  [the longest x1 376 us: local(): lax.all_to_all(task_vectors, 'ckpt', split_axis=1, concat_axis=0, tiled=T...]
    pallas_call x0 -> x1, Pallas kernels: none -> 382 us  [local(): pl.pallas_call(functools.partial(merge_kernel, T, S, R, min(W, 256)), out...]
    unnamed x1 -> x0, other arithmetic: 99.6 us -> none
    unnamed x6 -> x1, local copies, waits for them, and re-layouts: 82.6 us -> 7.89 us
    reduce_sum x2 -> x0, other arithmetic: 39 us -> none  [the longest x1 25.8 us: local_mean(): agree_count = jnp.sum(agreeing.astype(jnp.float32), axis=0)]
    all_to_all x2 -> x0, local copies, waits for them, and re-layouts: 37.4 us -> none  [the longest x1 28.2 us: local(): lax.all_to_all(task_vectors, 'ckpt', split_axis=1, concat_axis=0, tiled=T...]
    add x1 -> x0, other arithmetic: 11.9 us -> none  [local(): return base_weight + disjoint]
where the time goes in v1:
time: 390 us
  Pallas kernels  382 us (98%)
  local copies, waits for them, and re-layouts  7.89 us (2%)
    pallas_call x1, Pallas kernels, local(): pl.pallas_call(functools.partial(merge_kernel, T, S, R, min(W, 256)), out...  382 us
    unnamed x1, local copies, waits for them, and re-layouts  7.89 us

profile of v1, /device:TPU:0, one launch (start us, length us, event | category | flops | bytes accessed | tf_op | source)
XLA Modules:
  0.0 390.1 jit_solution(9648396485511479713)
XLA Ops:
  0.0 382.2 %merge_exchange.1 = f32[2,512,2048]{2,1,0:T(8,128)} custom-call(f32[4]{0:T(128)} %thr_ref.1, bf16[1,512,16384]{2,1,0:T(8,128)(2,1)} %x_ref.1, f32[2,512,2048]{2,1,0:T(8,128)} %bitcast.3), custom_call_target="tpu_custom_call" | custom-call | tf_op jit(solution)/shard_map/merge_exchange/pallas_call | solution.py:164
  382.2 7.9 %copy.5 = f32[1024,2048]{1,0:T(8,128)} copy(f32[1024,2048]{1,0:T(8,128)} %bitcast.2) | data formatting | bytes 16777216

commit v2 on v1

--- a/solution.py
+++ b/solution.py
@@ -15,9 +15,9 @@
 
 def merge_kernel(
     T, S, R, cw,
-    thr_ref, x_ref, base_ref, out_ref,
-    stage, recv, buf,
-    s1_send, s1_recv, s2_send, s2_recv, own_sem, base_sem, out_sem,
+    thr_ref, x_ref, base_ref, buf,
+    stage, recv, thr,
+    s1_send, s1_recv, s2_send, s2_recv, own_sem, base_sem, thr_sem,
 ):
     g = S // T
     RB, W = stage.shape[1], stage.shape[2]
@@ -29,6 +29,8 @@
         x_ref.at[0, :, pl.ds(pl.multiple_of(s * W, W), W)], stage.at[s], own_sem
     )
     base_in = pltpu.make_async_copy(base_ref, buf, base_sem)
+    thr_in = pltpu.make_async_copy(thr_ref, thr, thr_sem)
+    thr_in.start()
     own.start()
     base_in.start()
 
@@ -46,22 +48,24 @@
     def rows_of(j):
         return pl.ds(pl.multiple_of(j * R, R), R)
 
-    def plane_copy(j, d):
-        c = lax.rem(s + d, S)
+    mine = lax.div(s, g)
+    offsets = [0, T // 2] + [e for e in range(1, T) if e != T // 2]
+
+    def plane_copy(j, e, q):
+        c = lax.rem(mine + e, T) * g + lax.rem(lax.rem(s, g) + q, g)
         return pltpu.make_async_remote_copy(
             src_ref=x_ref.at[0, rows_of(j), pl.ds(pl.multiple_of(c * W, W), W)],
             dst_ref=stage.at[s, rows_of(j)],
             send_sem=s1_send.at[j],
-            recv_sem=s1_recv.at[j],
+            recv_sem=s1_recv.at[j, mine],
             device_id=(t, c),
             device_id_type=MESH,
         )
 
-    def line_copy(j, d):
-        k = lax.rem(t + d, T)
+    def line_copy(j, k):
         return pltpu.make_async_remote_copy(
             src_ref=stage.at[pl.ds(k * g, g), rows_of(j)],
-            dst_ref=recv.at[T - d - 1, :, rows_of(j)],
+            dst_ref=recv.at[lax.rem(t - k - 1 + T, T), :, rows_of(j)],
             send_sem=s2_send.at[j],
             recv_sem=s2_recv.at[j],
             device_id=(k, s),
@@ -69,20 +73,28 @@
         )
 
     def plane_start(j):
-        for d in range(S - 1, 0, -1):
-            plane_copy(j, d).start()
-
-    def plane_wait(sem, j):
+        for e in offsets[1:] + offsets[:1]:
+            for q in range(g):
+                if e or q:
+                    plane_copy(j, e, q).start()
+
+    def plane_arrived(j, e):
+        count = g if e else g - 1
+        if count:
+            part = stage.at[pl.ds(0, count), rows_of(j)]
+            sem = s1_recv.at[j, lax.rem(mine + e, T)]
+            pltpu.make_async_copy(part, part, sem).wait()
+
+    def plane_sent(j):
         part = stage.at[pl.ds(0, S - 1), rows_of(j)]
-        pltpu.make_async_copy(part, part, sem.at[j]).wait()
+        pltpu.make_async_copy(part, part, s1_send.at[j]).wait()
 
     def line_wait(sem, j):
         part = recv.at[:, :, rows_of(j)]
         pltpu.make_async_copy(part, part, sem.at[j]).wait()
 
-    limits = [thr_ref[lax.rem(t + d, T)] for d in range(T)]
-
     def mean_rows(j):
+        limits = [thr[lax.rem(t + d, T)] for d in range(T)]
         rows = rows_of(j)
 
         def cols_step(q, carry):
@@ -111,24 +123,26 @@
     def finish(j):
         line_wait(s2_recv, j)
         mean_rows(j)
-        pltpu.make_async_copy(
-            buf.at[:, rows_of(j)], out_ref.at[:, rows_of(j)], out_sem
-        ).start()
 
     ahead = min(AHEAD, N)
     for j in range(ahead):
         plane_start(j)
     own.wait()
     base_in.wait()
+    thr_in.wait()
 
     def step(j, carry):
         @pl.when(j + ahead < N)
         def _():
             plane_start(j + ahead)
 
-        plane_wait(s1_recv, j)
-        for d in range(T - 1, 0, -1):
-            line_copy(j, d).start()
+        for e in offsets:
+            k = lax.rem(mine + e, T)
+            plane_arrived(j, e)
+
+            @pl.when(k != t)
+            def _():
+                line_copy(j, k).start()
 
         @pl.when(j >= LAG)
         def _():
@@ -145,12 +159,11 @@
     lax.fori_loop(N - LAG, N, tail, 0)
 
     def drain(j, carry):
-        plane_wait(s1_send, j)
+        plane_sent(j)
         line_wait(s2_send, j)
         return carry
 
     lax.fori_loop(0, N, drain, 0)
-    pltpu.make_async_copy(buf, out_ref, out_sem).wait()
 
 
 def local(task_vectors, thresholds, base_weight):
@@ -163,19 +176,19 @@
     N = RB // R
     merged = pl.pallas_call(
         functools.partial(merge_kernel, T, S, R, min(W, 256)),
-        out_shape=jax.ShapeDtypeStruct((g, RB, W), jnp.float32),
+        out_shape=pltpu.VMEM((g, RB, W), jnp.float32),
         in_specs=[
-            pl.BlockSpec(memory_space=pltpu.SMEM),
-            pl.BlockSpec(memory_space=pl.ANY),
-            pl.BlockSpec(memory_space=pl.ANY),
+            pl.BlockSpec(memory_space=pltpu.HBM),
+            pl.BlockSpec(memory_space=pltpu.HBM),
+            pl.BlockSpec(memory_space=pltpu.HBM),
         ],
-        out_specs=pl.BlockSpec(memory_space=pl.ANY),
+        out_specs=pl.BlockSpec(memory_space=pltpu.VMEM),
         scratch_shapes=[
             pltpu.VMEM((S, RB, W), jnp.bfloat16),
             pltpu.VMEM((T - 1, g, RB, W), jnp.bfloat16),
-            pltpu.VMEM((g, RB, W), jnp.float32),
+            pltpu.SMEM((T,), jnp.float32),
             pltpu.SemaphoreType.DMA((N,)),
-            pltpu.SemaphoreType.DMA((N,)),
+            pltpu.SemaphoreType.DMA((N, T)),
             pltpu.SemaphoreType.DMA((N,)),
             pltpu.SemaphoreType.DMA((N,)),
             pltpu.SemaphoreType.DMA,
@@ -183,7 +196,7 @@
             pltpu.SemaphoreType.DMA,
         ],
         compiler_params=pltpu.CompilerParams(
-            collective_id=0, has_side_effects=True, vmem_limit_bytes=60 * 1024 * 1024
+            collective_id=0, has_side_effects=True, vmem_limit_bytes=40 * 1024 * 1024
         ),
         name="merge_exchange",
     )(thresholds, task_vectors, base_weight.reshape(g, RB, W))

time: 390 us -> 383 us (0.982)
  Pallas kernels: 382 us -> 378 us
    pallas_call x1, Pallas kernels: 382 us -> 378 us  [local(): pl.pallas_call(functools.partial(merge_kernel, T, S, R, min(W, 256)), out...]
    unnamed x1 -> x3, local copies, waits for them, and re-layouts: 7.89 us -> 4.05 us
where the time goes in v2:
time: 383 us; the launch traced here: 382 us
  Pallas kernels  378 us (99%)
  local copies, waits for them, and re-layouts  4.05 us (1%)
    pallas_call x1, Pallas kernels, local(): pl.pallas_call(functools.partial(merge_kernel, T, S, R, min(W, 256)), out...  378 us

profile of v2, /device:TPU:0, one launch (start us, length us, event | category | flops | bytes accessed | tf_op | source)
XLA Modules:
  0.0 382.0 jit_solution(6419494673577079475)
XLA Ops:
  0.0 0.0 copy-start
  0.0 0.7 copy-done
  0.7 377.9 %merge_exchange.1 = f32[2,512,2048]{2,1,0:T(8,128)S(1)} custom-call(f32[4]{0:T(128)S(1)} %copy-done, bf16[1,512,16384]{2,1,0:T(8,128)(2,1)} %x_ref.1, f32[2,512,2048]{2,1,0:T(8,128)} %bitcast.3), custom_call_target="tpu_custom_call" | custom-call | tf_op jit(solution)/shard_map/merge_exchange/pallas_call | solution.py:177
  378.6 3.4 copy.5
Async XLA Ops:
  0.0 0.7 copy-start

commit v3 on v2

--- a/solution.py
+++ b/solution.py
@@ -8,9 +8,10 @@
 from jax.sharding import PartitionSpec as P
 
 MESH = pl.DeviceIdType.MESH
+VMEM_BYTES = 67043328
 CHUNK = 16
 AHEAD = 3
-LAG = 2
+LAG = 4
 
 
 def merge_kernel(
@@ -49,10 +50,15 @@
         return pl.ds(pl.multiple_of(j * R, R), R)
 
     mine = lax.div(s, g)
-    offsets = [0, T // 2] + [e for e in range(1, T) if e != T // 2]
+    sign = 2 * lax.rem(mine, 2) - 1
+    offsets = [(0, 0)]
+    if T > 1:
+        offsets.append((1, T // 2))
+    for i in range(1, (T + 1) // 2):
+        offsets += [(1, T - sign * i), (1, T + sign * i)]
 
     def plane_copy(j, e, q):
-        c = lax.rem(mine + e, T) * g + lax.rem(lax.rem(s, g) + q, g)
+        c = lax.rem(mine + e[1], T) * g + lax.rem(lax.rem(s, g) + q, g)
         return pltpu.make_async_remote_copy(
             src_ref=x_ref.at[0, rows_of(j), pl.ds(pl.multiple_of(c * W, W), W)],
             dst_ref=stage.at[s, rows_of(j)],
@@ -75,14 +81,14 @@
     def plane_start(j):
         for e in offsets[1:] + offsets[:1]:
             for q in range(g):
-                if e or q:
+                if e[0] or q:
                     plane_copy(j, e, q).start()
 
     def plane_arrived(j, e):
-        count = g if e else g - 1
+        count = g if e[0] else g - 1
         if count:
             part = stage.at[pl.ds(0, count), rows_of(j)]
-            sem = s1_recv.at[j, lax.rem(mine + e, T)]
+            sem = s1_recv.at[j, lax.rem(mine + e[1], T)]
             pltpu.make_async_copy(part, part, sem).wait()
 
     def plane_sent(j):
@@ -137,7 +143,7 @@
             plane_start(j + ahead)
 
         for e in offsets:
-            k = lax.rem(mine + e, T)
+            k = lax.rem(mine + e[1], T)
             plane_arrived(j, e)
 
             @pl.when(k != t)
@@ -196,7 +202,7 @@
             pltpu.SemaphoreType.DMA,
         ],
         compiler_params=pltpu.CompilerParams(
-            collective_id=0, has_side_effects=True, vmem_limit_bytes=40 * 1024 * 1024
+            collective_id=0, has_side_effects=True, vmem_limit_bytes=VMEM_BYTES - g * RB * W * 4
         ),
         name="merge_exchange",
     )(thresholds, task_vectors, base_weight.reshape(g, RB, W))

time: 383 us -> 376 us (0.982)
  Pallas kernels: 378 us -> 368 us
    pallas_call x1, Pallas kernels: 378 us -> 368 us  [local(): pl.pallas_call(functools.partial(merge_kernel, T, S, R, min(W, 256)), out...]
where the time goes in v3:
time: 376 us; the launch traced here: 371 us
  Pallas kernels  368 us (98%)
    pallas_call x1, Pallas kernels, local(): pl.pallas_call(functools.partial(merge_kernel, T, S, R, min(W, 256)), out...  368 us

profile of v3, /device:TPU:0, one launch (start us, length us, event | category | flops | bytes accessed | tf_op | source)
XLA Modules:
  0.0 371.3 jit_solution(18289959874635443275)
XLA Ops:
  0.0 367.9 %merge_exchange.1 = f32[2,512,2048]{2,1,0:T(8,128)S(1)} custom-call(f32[4]{0:T(128)} %thr_ref.1, bf16[1,512,16384]{2,1,0:T(8,128)(2,1)} %x_ref.1, f32[2,512,2048]{2,1,0:T(8,128)} %bitcast.3), custom_call_target="tpu_custom_call" | custom-call | tf_op jit(solution)/shard_map/merge_exchange/pallas_call | solution.py:183
  367.9 3.4 copy.5
